TPU v7x, 128 devices: a whole 4x4x4 slice. The times are simulated.
128 devices in a mesh: row: 8 (over y, core), col: 16 (over z, x).
Axes of the slice: x: 4, y: 4, z: 4, core: 2. Of those that a mesh axis runs over, the one named last changes fastest.
Arguments:
- kernel_panel: float32 [64, 32768], P(None, ('row', 'col')), may hold values from -4 to 16, as said below
- kernel_slab: float32 [32768, 4096], P('row', 'col'), may hold values from -4 to 20, as said below
- targets: float32 [256, 32768], P(None, ('row', 'col')), may hold values from -6 to 6
Outputs:
- updated_slab: float32 [32768, 4096], P('row', 'col')
- solved_targets: float32 [256, 32768], P('col', 'row')
- panel_factor: float32 [64, 32768], P(None, ('row', 'col'))
Inputs may be any that keep to these rules, and one draw needn't show every extreme that they name: kernel_panel[:, 0:64] is symmetric and positive definite. `kernel_slab`: rows 0 to 63 equal kernel_panel[:, 32768 - 4096 : 32768]; the last 4096 rows form a symmetric matrix.
All inputs are finite; a program needn't handle non-finite values.
Results may differ from a plain program's by a relative error of at most 0.00018.
Values sent between devices are 32-bit elements; how exact they have to be, the bound alone decides.
No kernel may reach another device: no remote copies, remote signals or barrier semaphores. Data moves between devices by JAX's collectives and lax.ppermute only.
A program may use at most 64 MiB of HBM per device.

v0:
```python
import jax
import jax.numpy as jnp
from jax import lax
from jax.sharding import PartitionSpec as P


def spread(block, axis, source):
    block = jnp.where(lax.axis_index(axis) == source, block, jnp.zeros_like(block))
    return lax.psum(block, axis)


def lower_solve(factor, values):
    return jax.scipy.linalg.solve_triangular(factor, values, lower=True)


def body(kernel_panel, kernel_slab, targets):
    highest = lax.Precision.HIGHEST
    panel_width = kernel_panel.shape[0]
    row_count = lax.axis_size("row")
    row_index = lax.axis_index("row")
    flat_index = lax.axis_index(("row", "col"))
    corner_rows = jnp.concatenate([kernel_panel[:, :panel_width], targets[:, :panel_width]], 0)
    shared = spread(corner_rows, ("row", "col"), 0)
    lower_factor = jnp.linalg.cholesky(shared[:panel_width])
    panel_factor = lower_solve(lower_factor, kernel_panel)
    gathered = lax.all_gather(panel_factor, "col", axis=1, tiled=True)
    slab_factor = spread(panel_factor, "row", row_count - 1)
    product = lax.dot_general(
        gathered,
        slab_factor,
        (((0,), (0,)), ((), ())),
        precision=highest,
        preferred_element_type=jnp.float32,
    )
    update = kernel_slab - product
    head_rows = jnp.where(row_index == 0, slab_factor, update[:panel_width])
    updated_slab = jnp.concatenate([head_rows, update[panel_width:]], 0)
    solved_lead = lower_solve(lower_factor, shared[panel_width:].T).T
    result = targets - jnp.dot(
        solved_lead, panel_factor, precision=highest, preferred_element_type=jnp.float32
    )
    head_cols = jnp.where(flat_index == 0, solved_lead, result[:, :panel_width])
    result = jnp.concatenate([head_cols, result[:, panel_width:]], 1)
    solved_targets = lax.all_to_all(result, "col", split_axis=0, concat_axis=1, tiled=True)
    return (updated_slab, solved_targets, panel_factor)


def solution(mesh):
    in_specs = (P(None, ("row", "col")), P("row", "col"), P(None, ("row", "col")))
    out_specs = (P("row", "col"), P("col", "row"), P(None, ("row", "col")))
    return jax.shard_map(body, mesh=mesh, in_specs=in_specs, out_specs=out_specs, check_vma=False)
```

profile of v0, /device:TPU:0, one launch (start us, length us, event | category | flops | bytes accessed | tf_op | source)
XLA Modules:
  0.0 286.8 jit_solution(15664791899250229156)
XLA Ops:
  7.2 0.0 all-reduce.3.cloned.1.call-start
  7.2 0.8 slice.34
  8.0 0.1 copy.22
  8.1 1.1 copy.17
  9.2 0.7 maximum_select_fusion
  9.9 0.0 all-reduce.3.cloned.1.call-update
  9.9 0.0 all-reduce.5.cloned.1.call-start
  10.0 143.3 %all-reduce.3.cloned.1.call-done = f32[320,64]{0,1:T(8,128)} async-done(((f32[320,64]{0,1:T(8,128)}), f32[320,64]{0,1:T(8,128)}) %all-reduce.3.cloned.1.call-update) | async-done | bytes 81936 | tf_op jit(solution)/shard_map/psum | solution.py:9
  153.3 0.8 slice.43
  154.1 0.1 copy.18
  154.1 0.8 fusion.5
  154.9 5.8 %cholesky.18 = f32[64,64]{1,0:T(8,128)S(1)} custom-call(f32[64,64]{1,0:T(8,128)S(1)} %fusion.5), custom_call_target="Cholesky" | custom-call | tf_op jit(solution)/shard_map/jit(cholesky)/cholesky | solution.py:24
  160.8 0.6 compare_reduce_fusion
  161.4 0.7 fusion.1
  162.1 4.9 %custom-call.7 = f32[1,64,64]{1,2,0:T(8,128)S(1)} custom-call(f32[1,64,64]{2,1,0:T(8,128)S(1)} %fusion.1), custom_call_target="InvertDiagBlocksLowerTriangular" | custom-call | tf_op jit(solution)/shard_map/jit(_solve_triangular)/triangular_solve | solution.py:13
  167.0 1.8 broadcast_select_fusion
  168.8 0.0 all-reduce.5.cloned.1.call-update
  168.8 0.0 all-gather.2.cloned.1.call-start
  168.8 0.7 all-gather.2.cloned.1.call-update
  169.5 1.2 fusion
  170.7 1.3 convolution_subtract_fusion.1
  172.0 0.8 copy.20
  172.9 5.6 %all-to-all-start = ((f32[16,16,256]{2,1,0:T(8,128)}), f32[16,16,256]{2,1,0:T(8,128)S(1)}, u32[]{:S(2)}, u32[]{:S(2)}) async-start(f32[16,16,256]{2,1,0:T(8,128)} %bitcast.7), calls=%async_computation | async-start | bytes 524288 | tf_op jit(solution)/shard_map/all_to_all | solution.py:44
  178.5 8.7 %all-to-all-done = f32[16,16,256]{2,1,0:T(8,128)S(1)} async-done(((f32[16,16,256]{2,1,0:T(8,128)}), f32[16,16,256]{2,1,0:T(8,128)S(1)}, u32[]{:S(2)}, u32[]{:S(2)}) %all-to-all-start) | async-done | bytes 262176 | tf_op jit(solution)/shard_map/all_to_all | solution.py:44
  187.2 0.7 copy.23
  187.9 38.0 %all-reduce.5.cloned.1.call-done = f32[64,256]{1,0:T(8,128)} async-done(((f32[64,256]{1,0:T(8,128)}), f32[64,256]{1,0:T(8,128)}) %all-reduce.5.cloned.1.call-update) | async-done | bytes 65552 | tf_op jit(solution)/shard_map/psum | solution.py:9
  225.9 45.2 %all-gather.2.cloned.1.call-done = f32[64,4096]{1,0:T(8,128)} async-done(((f32[64,256]{1,0:T(8,128)}), f32[64,4096]{1,0:T(8,128)}) %all-gather.2.cloned.1.call-update) | async-done | bytes 1048592 | tf_op jit(solution)/shard_map/all_gather | solution.py:26
  271.1 6.0 %convolution_subtract_fusion = f32[4096,256]{1,0:T(8,128)S(1)} fusion(f32[4096,256]{1,0:T(8,128)} %param.6, f32[64,4096]{1,0:T(8,128)} %all-gather.2.cloned.1.call-done, f32[64,256]{1,0:T(8,128)} %all-reduce.5.cloned.1.call-done), kind=kOutput, calls=%fused_computation | convolution fusion | flops 806354944 | bytes 9502720 | tf_op jit(solution)/shard_map/dot_general | solution.py:28
  277.1 0.0 copy-start
  277.1 0.3 slice.45
  277.4 0.6 copy-done
  278.0 2.3 pad_maximum_fusion
  (6 shorter events, 0.1 us)
Async XLA Ops:
  7.2 146.1 %all-reduce.3.cloned.1.call-start = ((), (), s32[]{:S(2)}) async-start(), calls=%async_computation.1 | async-start | bytes 196608 | tf_op jit(solution)/shard_map/psum | solution.py:9
  9.9 216.0 %all-reduce.5.cloned.1.call-start = ((), (), s32[]{:S(2)}) async-start(), calls=%async_computation.2 | async-start | bytes 131072 | tf_op jit(solution)/shard_map/psum | solution.py:9
  168.8 102.3 %all-gather.2.cloned.1.call-start = ((), (), s32[]{:S(2)}) async-start(), calls=%async_computation.3 | async-start | bytes 1114112 | tf_op jit(solution)/shard_map/all_gather | solution.py:26
  172.9 14.3 %all-to-all-start = ((f32[16,16,256]{2,1,0:T(8,128)}), f32[16,16,256]{2,1,0:T(8,128)S(1)}, u32[]{:S(2)}, u32[]{:S(2)}) async-start(f32[16,16,256]{2,1,0:T(8,128)} %bitcast.7), calls=%async_computation | async-start | bytes 524288 | tf_op jit(solution)/shard_map/all_to_all | solution.py:44
  277.1 0.8 copy-start
Sparse Core Ops, SparseCore 0:
  13.3 139.9 all-reduce.2
  168.9 56.9 all-reduce.4
  228.6 42.4 all-gather.1
where the time goes:
time: 287 us
  waiting for transfers between devices  236 us (82%)
  other arithmetic  15.9 us (6%)
  between operations  13.9 us (5%)
  matrix products  10.2 us (4%)
  starting transfers between devices  5.75 us (2%)
  local copies, waits for them, and re-layouts  5.16 us (2%)
    psum x2, waiting for transfers between devices, spread(): return lax.psum(block, axis)  181 us
    all_gather x1, waiting for transfers between devices, body(): gathered = lax.all_gather(panel_factor, 'col', axis=1, tiled=True)  45.2 us
    all_to_all x1, waiting for transfers between devices, body(): lax.all_to_all(result, 'col', split_axis=0, concat_axis=1, tiled=True)  8.69 us
    another operation x3, other arithmetic, body(): lower_factor = jnp.linalg.cholesky(shared[:panel_width])  6.52 us
    dot_general x1, matrix products, body(): lax.dot_general(gathered, slab_factor, (((0,), (0,)), ((), ())), precisio...  6 us
  transfers between devices with their start and end apart: 4, of which 4 were waited for; matrix products, arithmetic and copies ran while one was open for 1% of the time, Pallas kernels for 0%

commit v1 on v0

--- a/solution.py
+++ b/solution.py
@@ -6,7 +6,7 @@
 
 def spread(block, axis, source):
     block = jnp.where(lax.axis_index(axis) == source, block, jnp.zeros_like(block))
-    return lax.psum(block, axis)
+    return jnp.sum(lax.all_gather(block, axis), axis=0)
 
 
 def lower_solve(factor, values):

time: 287 us -> 165 us (0.57)
  waiting for transfers between devices: 236 us -> 98.3 us
  blocking collectives: 0 us -> 13.1 us
  other arithmetic: 15.9 us -> 20.4 us
    psum x2 -> x0, waiting for transfers between devices: 181 us -> none  [spread(): return lax.psum(block, axis)]
    all_gather x0 -> x1, waiting for transfers between devices: none -> 77.5 us  [spread(): return jnp.sum(lax.all_gather(block, axis), axis=0)]
    all_gather x1, waiting for transfers between devices: 45.2 us -> 20.7 us  [body(): gathered = lax.all_gather(panel_factor, 'col', axis=1, tiled=True)]
    all_gather x0 -> x1, blocking collectives: none -> 13.1 us  [spread(): return jnp.sum(lax.all_gather(block, axis), axis=0)]
    all_to_all x1, waiting for transfers between devices: 8.69 us -> 0.01 us  [body(): lax.all_to_all(result, 'col', split_axis=0, concat_axis=1, tiled=True)]
    reduce_sum x0 -> x2, other arithmetic: none -> 5.3 us  [spread(): return jnp.sum(lax.all_gather(block, axis), axis=0)]
  transfers between devices with their start and end apart: 4 -> 3, of which waited for: 4 -> 2; matrix products, arithmetic and copies ran while one was open for 1% -> 2% of each run, Pallas kernels for 0% -> 0%
where the time goes in v1:
time: 165 us
  waiting for transfers between devices  98.3 us (60%)
  other arithmetic  20.4 us (12%)
  between operations  14.2 us (9%)
  blocking collectives  13.1 us (8%)
  matrix products  8.43 us (5%)
  starting transfers between devices  6.5 us (4%)
  local copies, waits for them, and re-layouts  4.03 us (2%)
    all_gather x1, waiting for transfers between devices, spread(): return jnp.sum(lax.all_gather(block, axis), axis=0)  77.5 us
    all_gather x1, waiting for transfers between devices, body(): gathered = lax.all_gather(panel_factor, 'col', axis=1, tiled=True)  20.7 us
    all_gather x1, blocking collectives, spread(): return jnp.sum(lax.all_gather(block, axis), axis=0)  13.1 us
    another operation x3, other arithmetic, body(): lower_factor = jnp.linalg.cholesky(shared[:panel_width])  6.52 us
    all_to_all x1, starting transfers between devices, body(): lax.all_to_all(result, 'col', split_axis=0, concat_axis=1, tiled=True)  6.42 us
    dot_general x1, matrix products, body(): lax.dot_general(gathered, slab_factor, (((0,), (0,)), ((), ())), precisio...  5.98 us
    another operation x2, other arithmetic, lower_solve(): return jax.scipy.linalg.solve_triangular(factor, values, lower=True)  5.55 us
    reduce_sum x2, other arithmetic, spread(): return jnp.sum(lax.all_gather(block, axis), axis=0)  5.3 us
  transfers between devices with their start and end apart: 3, of which 2 were waited for; matrix products, arithmetic and copies ran while one was open for 2% of the time, Pallas kernels for 0%

profile of v1, /device:TPU:0, one launch (start us, length us, event | category | flops | bytes accessed | tf_op | source)
XLA Modules:
  0.0 165.0 jit_solution(8971502408998451964)
XLA Ops:
  7.2 0.0 all-gather.4.cloned.1.call-start
  7.2 1.1 copy.17
  8.3 0.8 slice.34
  9.1 0.1 copy.25
  9.2 0.7 maximum_select_fusion
  9.9 0.0 all-gather.4.cloned.1.call-update
  9.9 0.0 all-gather.6.cloned.1.call-start
  10.0 0.0 copy-start
  10.0 77.5 %all-gather.4.cloned.1.call-done = f32[128,320,64]{1,2,0:T(8,128)} async-done(((f32[1,320,64]{1,2,0:T(8,128)}), f32[128,320,64]{1,2,0:T(8,128)}) %all-gather.4.cloned.1.call-update) | async-done | bytes 10485776 | tf_op jit(solution)/shard_map/all_gather | solution.py:9
  87.5 5.3 %reduce_sum.18 = f32[320,64]{0,1:T(8,128)S(1)} reduce(f32[128,320,64]{1,2,0:T(8,128)} %all-gather.4.cloned.1.call-done, f32[]{:T(128)} %constant.56.clone.1), dimensions={0}, to_apply=%region_0.1 | reduce | flops 2600960 | bytes 10567684 | tf_op jit(solution)/shard_map/reduce_sum | solution.py:9
  92.7 0.1 copy.27
  92.8 5.8 %cholesky.18 = f32[64,64]{1,0:T(8,128)S(1)} custom-call(f32[64,64]{1,0:T(8,128)S(1)} %fusion.6), custom_call_target="Cholesky" | custom-call | tf_op jit(solution)/shard_map/jit(cholesky)/cholesky | solution.py:24
  98.7 0.6 compare_reduce_fusion
  99.4 0.7 fusion.2
  100.0 4.9 %custom-call.7 = f32[1,64,64]{1,2,0:T(8,128)S(1)} custom-call(f32[1,64,64]{2,1,0:T(8,128)S(1)} %fusion.2), custom_call_target="InvertDiagBlocksLowerTriangular" | custom-call | tf_op jit(solution)/shard_map/jit(_solve_triangular)/triangular_solve | solution.py:13
  104.9 0.0 copy-done
  104.9 0.9 broadcast_select_fusion
  105.8 0.0 all-gather.6.cloned.1.call-update
  105.8 0.1 slice.46
  105.9 0.1 copy.28
  106.0 0.3 fusion
  106.3 1.3 convolution_subtract_fusion.1
  107.7 0.8 copy.22
  108.5 6.4 %all-to-all-start = ((f32[16,16,256]{2,1,0:T(8,128)}), f32[16,16,256]{2,1,0:T(8,128)S(1)}, u32[]{:S(2)}, u32[]{:S(2)}) async-start(f32[16,16,256]{2,1,0:T(8,128)} %bitcast.10), calls=%async_computation | async-start | bytes 524288 | tf_op jit(solution)/shard_map/all_to_all | solution.py:44
  114.9 13.1 %all-gather = f32[512,256]{1,0:T(8,128)S(1)} all-gather(f32[64,256]{1,0:T(8,128)S(1)} %get-tuple-element.4), channel_id=2, replica_groups=mesh['row'=8,'col'=16] {'row'}, dimensions={0}, use_global_device_ids=true | all-gather | bytes 589824 | tf_op jit(solution)/shard_map/all_gather | solution.py:9
  128.1 0.0 all-to-all-done
  128.1 0.7 copy.29
  128.8 20.7 %all-gather.6.cloned.1.call-done = f32[64,4096]{1,0:T(8,128)} async-done(((f32[64,256]{1,0:T(8,128)}), f32[64,4096]{1,0:T(8,128)}) %all-gather.6.cloned.1.call-update) | async-done | bytes 1048592 | tf_op jit(solution)/shard_map/all_gather | solution.py:26
  149.6 6.0 %convolution_subtract_fusion = f32[4096,256]{1,0:T(8,128)S(1)} fusion(f32[4096,256]{1,0:T(8,128)} %param.6, f32[64,4096]{1,0:T(8,128)} %all-gather.6.cloned.1.call-done, f32[64,256]{1,0:T(8,128)S(1)} %reduce_sum.19), kind=kOutput, calls=%fused_computation | convolution fusion | flops 806354944 | bytes 9502720 | tf_op jit(solution)/shard_map/dot_general | solution.py:28
  155.6 0.3 slice.45
  155.8 2.3 %pad_maximum_fusion = f32[4096,256]{1,0:T(8,128)} fusion(f32[4032,256]{1,0:T(8,128)S(1)} %slice.45, f32[64,256]{1,0:T(8,128)S(1)} %slice_select_fusion.1), kind=kLoop, calls=%fused_computation.1 | loop fusion | flops 1048576 | bytes 8388608 | tf_op jit(solution)/shard_map/concatenate | solution.py:37
  (9 shorter events, 0.1 us)
Async XLA Ops:
  7.2 80.3 %all-gather.4.cloned.1.call-start = ((), (), s32[]{:S(2)}) async-start(), calls=%async_computation.1 | async-start | bytes 12681216 | tf_op jit(solution)/shard_map/all_gather | solution.py:9
  9.9 139.6 %all-gather.6.cloned.1.call-start = ((), (), s32[]{:S(2)}) async-start(), calls=%async_computation.2 | async-start | bytes 1114112 | tf_op jit(solution)/shard_map/all_gather | solution.py:26
  10.0 94.9 %copy-start = (f32[64,256]{1,0:T(8,128)S(1)}, f32[64,256]{1,0:T(8,128)}, u32[]{:S(2)}) copy-start(f32[64,256]{1,0:T(8,128)} %param.5) | copy-start | bytes 196612
  108.5 19.6 %all-to-all-start = ((f32[16,16,256]{2,1,0:T(8,128)}), f32[16,16,256]{2,1,0:T(8,128)S(1)}, u32[]{:S(2)}, u32[]{:S(2)}) async-start(f32[16,16,256]{2,1,0:T(8,128)} %bitcast.10), calls=%async_computation | async-start | bytes 524288 | tf_op jit(solution)/shard_map/all_to_all | solution.py:44
Sparse Core Ops, SparseCore 0:
  11.7 75.7 all-gather.3
  106.0 43.5 all-gather.5
